TPU v7x, 32 devices: a whole 2x2x4 slice. The times are simulated.
32 devices in a mesh: section: 4 (over x, core), tp: 8 (over z, y).
Axes of the slice: x: 2, y: 2, z: 4, core: 2. Of those that a mesh axis runs over, the one named last changes fastest.
Arguments:
- layer_inputs: bfloat16 [8, 512, 4096], P('section', None, 'tp'), may hold values from -6 to 6
- weights: bfloat16 [8, 4096, 4096], P('section', 'tp'), may hold values from -0.046875 to 0.046875
- input_basis: bfloat16 [8, 4096, 64], P('section', 'tp'), may hold values from -0.09375 to 0.09375
- output_basis: bfloat16 [8, 4096, 32], P('section', 'tp'), may hold values from -0.09375 to 0.09375
- queries: bfloat16 [8, 512, 2048], P('section', 'tp'), may hold values from -0.00390625 to 0.00390625
- top_cotangent: bfloat16 [512, 4096], replicated, may hold values from -6 to 6
- sequence_example: int32 [4], replicated, may hold values from 0 to 1
Outputs:
- scores: float32 [2, 512], P(None, 'tp')
All inputs are finite; a program needn't handle non-finite values.
Results may differ from a plain program's by a relative error of at most 0.0094.
Values may be sent and summed in bfloat16 or wider, within the bound.
A program may use at most 64 MiB of HBM per device.

v0:
```python
import jax
import jax.numpy as jnp
from jax import lax
from jax.sharding import PartitionSpec as P

SEQLEN = 128
SEQ_MB = 1
MB = 4
EXAMPLES = 2


def from_behind(value, axis, by):
    size = lax.axis_size(axis)
    pairs = [(i, i + by) for i in range(size) if 0 <= i + by < size]
    return lax.ppermute(value, axis, pairs)


def silu_parts(values):
    floats = values.astype(jnp.float32)
    logistic = jax.nn.sigmoid(floats)
    return ((floats * logistic).astype(jnp.bfloat16), logistic * (1.0 + floats * (1.0 - logistic)))


def contract_columns(portion, matrix):
    return lax.dot_general(
        portion, matrix, (((1,), (1,)), ((), ())), preferred_element_type=jnp.float32
    )


def outer_rows(out_feats, in_feats):
    joined = out_feats[:, :, :, None] * in_feats[:, :, None, :]
    return joined.reshape(joined.shape[0], joined.shape[1], -1)


def shards(
    layer_inputs, weights, input_basis, output_basis, queries, top_cotangent, sequence_example
):
    section_count = lax.axis_size("section")
    section_rank = lax.axis_index("section")
    tp_rank = lax.axis_index("tp")
    width_local = layer_inputs.shape[2]
    total_tokens = layer_inputs.shape[1]
    block_rows = SEQ_MB * SEQLEN
    activated, slopes = silu_parts(layer_inputs)
    partial_in = jnp.einsum(
        "ltd,ldr->tlr", activated, input_basis, preferred_element_type=jnp.float32
    )
    in_feats = lax.psum(partial_in.reshape(total_tokens, -1), "tp").reshape(partial_in.shape)
    example_index = jnp.arange(EXAMPLES, dtype=jnp.int32)
    is_top = section_rank == section_count - 1

    def fold_upper(portion):
        return contract_columns(portion, weights[1])

    def fold_lower(portion):
        return contract_columns(portion, weights[0])

    def tick(tick_index, state):
        outgoing, grads, stored = state
        micro_index = tick_index - (section_count - 1 - section_rank)
        valid = (micro_index >= 0) & (micro_index < MB)
        micro_clip = jnp.clip(micro_index, 0, MB - 1)
        first_row = micro_clip * block_rows
        slope_block = lax.dynamic_slice_in_dim(slopes, first_row, block_rows, 1)
        received = from_behind(outgoing, "section", -1)
        top_block = lax.dynamic_slice(
            top_cotangent, (first_row, tp_rank * width_local), (block_rows, width_local)
        )
        upper_own = jnp.where(is_top, top_block, received)
        upper_branch = fold_upper(lax.all_gather(upper_own, "tp", axis=1, tiled=True))
        middle_own = (upper_own.astype(jnp.float32) + slope_block[1] * upper_branch).astype(
            jnp.bfloat16
        )
        lower_branch = fold_lower(lax.all_gather(middle_own, "tp", axis=1, tiled=True))
        lower_own = (middle_own.astype(jnp.float32) + slope_block[0] * lower_branch).astype(
            jnp.bfloat16
        )
        cotangents = jnp.stack([middle_own, upper_own], 0)
        partial_out = jnp.einsum(
            "lrd,ldk->rlk", cotangents, output_basis, preferred_element_type=jnp.float32
        )
        out_feats = lax.psum(partial_out.reshape(block_rows, -1), "tp").reshape(partial_out.shape)
        in_block = lax.dynamic_slice_in_dim(in_feats, first_row, block_rows, 0)
        block_examples = jnp.repeat(
            lax.dynamic_slice_in_dim(sequence_example, micro_clip * SEQ_MB, SEQ_MB, 0), SEQLEN
        )
        selector = (example_index[:, None] == block_examples[None, :]).astype(
            jnp.float32
        ) * valid.astype(jnp.float32)
        grads = grads + jnp.einsum(
            "er,rlk->lek",
            selector,
            outer_rows(out_feats, in_block),
            precision=lax.Precision.HIGHEST,
        )
        return (lower_own, grads, stored)

    outgoing_init = jnp.zeros((block_rows, width_local), jnp.bfloat16)
    grads_init = jnp.zeros((2, EXAMPLES, queries.shape[2]), jnp.float32)
    stored_init = jnp.zeros((1,), jnp.bfloat16)
    final_out, grads, stored = lax.fori_loop(
        0, MB + section_count - 1, tick, (outgoing_init, grads_init, stored_init)
    )
    layer_scores = jnp.einsum(
        "lek,lqk->eq", grads, queries.astype(jnp.float32), precision=lax.Precision.HIGHEST
    )
    return lax.psum(layer_scores, "section")


def solution(mesh):
    placed = (
        P("section", None, "tp"),
        P("section", "tp", None),
        P("section", "tp", None),
        P("section", "tp", None),
        P("section", "tp", None),
        P(),
        P(),
    )
    return jax.shard_map(
        shards, mesh=mesh, in_specs=placed, out_specs=P(None, "tp"), check_vma=False
    )
```

profile of v0, /device:TPU:0, one launch (start us, length us, event | category | flops | bytes accessed | tf_op | source)
XLA Modules:
  0.0 749.2 jit_solution(505250659360147819)
XLA Ops:
  11.2 73.2 %all-reduce.2.cloned.1.call-done = f32[512,2,64]{0,2,1:T(8,128)} async-done(((f32[512,2,64]{0,2,1:T(8,128)}), f32[512,2,64]{0,2,1:T(8,128)}) %all-reduce.2.cloned.1.call-update) | async-done | bytes 262160 | tf_op jit(solution)/shard_map/psum | solution.py:48
  84.5 651.5 %while.18 = (s32[]{:T(128)}, bf16[128,512]{1,0:T(8,128)(2,1)S(1)}, f32[2,2,2048]{2,1,0:T(2,128)S(1)}, pred[]{:T(512)}, s32[]{:T(128)}, /*index=5*/bf16[512,4096]...) while((s32[]{:T(128)}, bf16[128,512]{1,0:T(8,128)(2,1)S(1)}, ...), condition=%wide.region_3.4_spmd.clone, body=%wide.region_1.3_spmd.clone.sunk | while | flops 1096048640 | bytes 25756184 | solution.py:101
  89.4 40.3 %all-gather.3.cloned.1.call-done = bf16[128,4096]{1,0:T(8,128)(2,1)} async-done(((bf16[128,512]{1,0:T(8,128)(2,1)}), bf16[128,4096]{1,0:T(8,128)(2,1)}) %all-gather.3.cloned.1.call-update) | async-done | bytes 1048592 | tf_op jit(solution)/shard_map/while/body/eval_jaxpr/all_gather | solution.py:70
  129.7 4.7 add_convert_fusion.4
  137.5 35.6 %psum.31 = f32[128,2,32]{0,2,1:T(8,128)S(1)} all-reduce(f32[128,2,32]{0,2,1:T(8,128)S(1)} %convolution_bitcast_fusion.5), channel_id=1, replica_groups=mesh['section'=4,'tp'=8] {'tp'}, use_global_device_ids=true, to_apply=%region_2.2 | all-reduce | flops 8192 | bytes 65536 | tf_op jit(solution)/shard_map/while/body/eval_jaxpr/psum | solution.py:82
  184.3 38.2 %all-gather.3.cloned.1.call-done = bf16[128,4096]{1,0:T(8,128)(2,1)} async-done(((bf16[128,512]{1,0:T(8,128)(2,1)}), bf16[128,4096]{1,0:T(8,128)(2,1)}) %all-gather.3.cloned.1.call-update) | async-done | bytes 1048592 | tf_op jit(solution)/shard_map/while/body/eval_jaxpr/all_gather | solution.py:70
  222.5 4.7 add_convert_fusion.4
  230.3 35.6 %psum.31 = f32[128,2,32]{0,2,1:T(8,128)S(1)} all-reduce(f32[128,2,32]{0,2,1:T(8,128)S(1)} %convolution_bitcast_fusion.5), channel_id=1, replica_groups=mesh['section'=4,'tp'=8] {'tp'}, use_global_device_ids=true, to_apply=%region_2.2 | all-reduce | flops 8192 | bytes 65536 | tf_op jit(solution)/shard_map/while/body/eval_jaxpr/psum | solution.py:82
  277.1 38.2 %all-gather.3.cloned.1.call-done = bf16[128,4096]{1,0:T(8,128)(2,1)} async-done(((bf16[128,512]{1,0:T(8,128)(2,1)}), bf16[128,4096]{1,0:T(8,128)(2,1)}) %all-gather.3.cloned.1.call-update) | async-done | bytes 1048592 | tf_op jit(solution)/shard_map/while/body/eval_jaxpr/all_gather | solution.py:70
  315.3 4.7 add_convert_fusion.4
  323.0 35.6 %psum.31 = f32[128,2,32]{0,2,1:T(8,128)S(1)} all-reduce(f32[128,2,32]{0,2,1:T(8,128)S(1)} %convolution_bitcast_fusion.5), channel_id=1, replica_groups=mesh['section'=4,'tp'=8] {'tp'}, use_global_device_ids=true, to_apply=%region_2.2 | all-reduce | flops 8192 | bytes 65536 | tf_op jit(solution)/shard_map/while/body/eval_jaxpr/psum | solution.py:82
  369.8 38.2 %all-gather.3.cloned.1.call-done = bf16[128,4096]{1,0:T(8,128)(2,1)} async-done(((bf16[128,512]{1,0:T(8,128)(2,1)}), bf16[128,4096]{1,0:T(8,128)(2,1)}) %all-gather.3.cloned.1.call-update) | async-done | bytes 1048592 | tf_op jit(solution)/shard_map/while/body/eval_jaxpr/all_gather | solution.py:70
  408.0 4.7 add_convert_fusion.4
  415.8 35.6 %psum.31 = f32[128,2,32]{0,2,1:T(8,128)S(1)} all-reduce(f32[128,2,32]{0,2,1:T(8,128)S(1)} %convolution_bitcast_fusion.5), channel_id=1, replica_groups=mesh['section'=4,'tp'=8] {'tp'}, use_global_device_ids=true, to_apply=%region_2.2 | all-reduce | flops 8192 | bytes 65536 | tf_op jit(solution)/shard_map/while/body/eval_jaxpr/psum | solution.py:82
  462.6 38.2 %all-gather.3.cloned.1.call-done = bf16[128,4096]{1,0:T(8,128)(2,1)} async-done(((bf16[128,512]{1,0:T(8,128)(2,1)}), bf16[128,4096]{1,0:T(8,128)(2,1)}) %all-gather.3.cloned.1.call-update) | async-done | bytes 1048592 | tf_op jit(solution)/shard_map/while/body/eval_jaxpr/all_gather | solution.py:70
  500.8 4.7 add_convert_fusion.4
  508.6 35.6 %psum.31 = f32[128,2,32]{0,2,1:T(8,128)S(1)} all-reduce(f32[128,2,32]{0,2,1:T(8,128)S(1)} %convolution_bitcast_fusion.5), channel_id=1, replica_groups=mesh['section'=4,'tp'=8] {'tp'}, use_global_device_ids=true, to_apply=%region_2.2 | all-reduce | flops 8192 | bytes 65536 | tf_op jit(solution)/shard_map/while/body/eval_jaxpr/psum | solution.py:82
  555.4 38.2 %all-gather.3.cloned.1.call-done = bf16[128,4096]{1,0:T(8,128)(2,1)} async-done(((bf16[128,512]{1,0:T(8,128)(2,1)}), bf16[128,4096]{1,0:T(8,128)(2,1)}) %all-gather.3.cloned.1.call-update) | async-done | bytes 1048592 | tf_op jit(solution)/shard_map/while/body/eval_jaxpr/all_gather | solution.py:70
  593.6 4.7 add_convert_fusion.4
  601.3 35.6 %psum.31 = f32[128,2,32]{0,2,1:T(8,128)S(1)} all-reduce(f32[128,2,32]{0,2,1:T(8,128)S(1)} %convolution_bitcast_fusion.5), channel_id=1, replica_groups=mesh['section'=4,'tp'=8] {'tp'}, use_global_device_ids=true, to_apply=%region_2.2 | all-reduce | flops 8192 | bytes 65536 | tf_op jit(solution)/shard_map/while/body/eval_jaxpr/psum | solution.py:82
  648.1 38.2 %all-gather.3.cloned.1.call-done = bf16[128,4096]{1,0:T(8,128)(2,1)} async-done(((bf16[128,512]{1,0:T(8,128)(2,1)}), bf16[128,4096]{1,0:T(8,128)(2,1)}) %all-gather.3.cloned.1.call-update) | async-done | bytes 1048592 | tf_op jit(solution)/shard_map/while/body/eval_jaxpr/all_gather | solution.py:70
  686.3 4.7 add_convert_fusion.4
  694.1 35.6 %psum.31 = f32[128,2,32]{0,2,1:T(8,128)S(1)} all-reduce(f32[128,2,32]{0,2,1:T(8,128)S(1)} %convolution_bitcast_fusion.5), channel_id=1, replica_groups=mesh['section'=4,'tp'=8] {'tp'}, use_global_device_ids=true, to_apply=%region_2.2 | all-reduce | flops 8192 | bytes 65536 | tf_op jit(solution)/shard_map/while/body/eval_jaxpr/psum | solution.py:82
  736.4 6.2 psum.28
  (153 shorter events, 104.5 us)
Async XLA Ops:
  6.5 729.4 %copy-start = (bf16[2,64,2048]{2,1,0:T(8,128)(2,1)S(1)}, bf16[2,64,2048]{2,1,0:T(8,128)(2,1)}, u32[]{:S(2)}) copy-start(bf16[2,64,2048]{2,1,0:T(8,128)(2,1)} %param.13) | copy-start | bytes 1572868
  6.5 77.9 %all-reduce.2.cloned.1.call-start = ((), (), s32[]{:S(2)}) async-start(), calls=%async_computation | async-start | bytes 524288 | tf_op jit(solution)/shard_map/psum | solution.py:48
  9.2 75.2 %copy-start.4 = (s32[4]{0:T(128)S(1)}, s32[4]{0:T(128)}, u32[]{:S(2)}) copy-start(s32[4]{0:T(128)} %param.15) | copy-start | bytes 52
  84.5 45.3 %all-gather.3.cloned.1.call-start = ((), (), s32[]{:S(2)}) async-start(), calls=%async_computation.1 | async-start | bytes 1179648 | tf_op jit(solution)/shard_map/while/body/eval_jaxpr/all_gather | solution.py:70
  84.5 3.2 collective-permute-start
  89.3 85.9 %all-gather.5.cloned.1.call-start = ((), (), s32[]{:S(2)}) async-start(), calls=%async_computation.2 | async-start | bytes 1179648 | tf_op jit(solution)/shard_map/while/body/eval_jaxpr/all_gather | solution.py:74
  179.3 43.2 %all-gather.3.cloned.1.call-start = ((), (), s32[]{:S(2)}) async-start(), calls=%async_computation.1 | async-start | bytes 1179648 | tf_op jit(solution)/shard_map/while/body/eval_jaxpr/all_gather | solution.py:70
  179.4 3.2 collective-permute-start
  184.3 83.7 %all-gather.5.cloned.1.call-start = ((), (), s32[]{:S(2)}) async-start(), calls=%async_computation.2 | async-start | bytes 1179648 | tf_op jit(solution)/shard_map/while/body/eval_jaxpr/all_gather | solution.py:74
  272.1 43.2 %all-gather.3.cloned.1.call-start = ((), (), s32[]{:S(2)}) async-start(), calls=%async_computation.1 | async-start | bytes 1179648 | tf_op jit(solution)/shard_map/while/body/eval_jaxpr/all_gather | solution.py:70
  272.2 3.2 collective-permute-start
  277.0 83.7 %all-gather.5.cloned.1.call-start = ((), (), s32[]{:S(2)}) async-start(), calls=%async_computation.2 | async-start | bytes 1179648 | tf_op jit(solution)/shard_map/while/body/eval_jaxpr/all_gather | solution.py:74
  364.9 43.2 %all-gather.3.cloned.1.call-start = ((), (), s32[]{:S(2)}) async-start(), calls=%async_computation.1 | async-start | bytes 1179648 | tf_op jit(solution)/shard_map/while/body/eval_jaxpr/all_gather | solution.py:70
  364.9 3.2 collective-permute-start
  369.8 83.7 %all-gather.5.cloned.1.call-start = ((), (), s32[]{:S(2)}) async-start(), calls=%async_computation.2 | async-start | bytes 1179648 | tf_op jit(solution)/shard_map/while/body/eval_jaxpr/all_gather | solution.py:74
  457.6 43.2 %all-gather.3.cloned.1.call-start = ((), (), s32[]{:S(2)}) async-start(), calls=%async_computation.1 | async-start | bytes 1179648 | tf_op jit(solution)/shard_map/while/body/eval_jaxpr/all_gather | solution.py:70
  457.7 3.2 collective-permute-start
  462.6 83.7 %all-gather.5.cloned.1.call-start = ((), (), s32[]{:S(2)}) async-start(), calls=%async_computation.2 | async-start | bytes 1179648 | tf_op jit(solution)/shard_map/while/body/eval_jaxpr/all_gather | solution.py:74
  550.4 43.2 %all-gather.3.cloned.1.call-start = ((), (), s32[]{:S(2)}) async-start(), calls=%async_computation.1 | async-start | bytes 1179648 | tf_op jit(solution)/shard_map/while/body/eval_jaxpr/all_gather | solution.py:70
  550.5 3.2 collective-permute-start
  555.3 83.7 %all-gather.5.cloned.1.call-start = ((), (), s32[]{:S(2)}) async-start(), calls=%async_computation.2 | async-start | bytes 1179648 | tf_op jit(solution)/shard_map/while/body/eval_jaxpr/all_gather | solution.py:74
  643.2 43.2 %all-gather.3.cloned.1.call-start = ((), (), s32[]{:S(2)}) async-start(), calls=%async_computation.1 | async-start | bytes 1179648 | tf_op jit(solution)/shard_map/while/body/eval_jaxpr/all_gather | solution.py:70
  643.2 3.2 collective-permute-start
  648.1 83.7 %all-gather.5.cloned.1.call-start = ((), (), s32[]{:S(2)}) async-start(), calls=%async_computation.2 | async-start | bytes 1179648 | tf_op jit(solution)/shard_map/while/body/eval_jaxpr/all_gather | solution.py:74
  (15 other events, 137.5 us)
Sparse Core Ops, SparseCore 0:
  10.7 73.7 all-reduce.1
  89.5 40.2 all-gather.2
  134.6 38.5 all-gather.4
  184.4 38.0 all-gather.2
  227.3 38.5 all-gather.4
  277.2 38.0 all-gather.2
  320.1 38.5 all-gather.4
  369.9 38.0 all-gather.2
  412.9 38.5 all-gather.4
  462.7 38.0 all-gather.2
  505.6 38.5 all-gather.4
  555.5 38.0 all-gather.2
  598.4 38.5 all-gather.4
  648.2 38.0 all-gather.2
  691.2 38.5 all-gather.4
where the time goes:
time: 750 us; the launch traced here: 749 us
  waiting for transfers between devices  356 us (47%)
  blocking collectives  255 us (34%)
  matrix products  85.2 us (11%)
  other arithmetic  18.8 us (3%)
  between operations  13.1 us (2%)
  local copies, waits for them, and re-layouts  9.96 us (1%)
  starting transfers between devices  9.6 us (1%)
    all_gather x7, waiting for transfers between devices, tick(): lax.all_gather(upper_own, 'tp', axis=1, tiled=True)  269 us
    psum x7, blocking collectives, tick(): lax.psum(partial_out.reshape(block_rows, -1), 'tp')  249 us
    psum x1, waiting for transfers between devices, shards(): lax.psum(partial_in.reshape(total_tokens, -1), 'tp')  73.2 us
    dot_general x14, matrix products, contract_columns(): lax.dot_general(portion, matrix, (((1,), (1,)), ((), ())), preferred_elem...  61.2 us
  transfers between devices with their start and end apart: 22, of which 15 were waited for; matrix products, arithmetic and copies ran while one was open for 5% of the time, Pallas kernels for 0%

commit v1 on v0

--- a/solution.py
+++ b/solution.py
@@ -79,7 +79,9 @@
         partial_out = jnp.einsum(
             "lrd,ldk->rlk", cotangents, output_basis, preferred_element_type=jnp.float32
         )
-        out_feats = lax.psum(partial_out.reshape(block_rows, -1), "tp").reshape(partial_out.shape)
+        out_feats = jnp.sum(
+            lax.all_gather(partial_out.reshape(block_rows, -1), "tp"), axis=0
+        ).reshape(partial_out.shape)
         in_block = lax.dynamic_slice_in_dim(in_feats, first_row, block_rows, 0)
         block_examples = jnp.repeat(
             lax.dynamic_slice_in_dim(sequence_example, micro_clip * SEQ_MB, SEQ_MB, 0), SEQLEN

time: 750 us -> 754 us (level)
  waiting for transfers between devices: 356 us -> 387 us
  blocking collectives: 255 us -> 228 us
    psum x7 -> x0, blocking collectives: 249 us -> none  [tick(): lax.psum(partial_out.reshape(block_rows, -1), 'tp')]
    all_gather x0 -> x7, blocking collectives: none -> 222 us  [tick(): lax.all_gather(partial_out.reshape(block_rows, -1), 'tp')]
    all_gather x7, waiting for transfers between devices: 0.12 us -> 19.5 us  [tick(): lax.all_gather(middle_own, 'tp', axis=1, tiled=True)]
    all_gather x7, waiting for transfers between devices: 269 us -> 280 us  [tick(): lax.all_gather(upper_own, 'tp', axis=1, tiled=True)]
  transfers between devices with their start and end apart: 22 -> 22, of which waited for: 15 -> 22; matrix products, arithmetic and copies ran while one was open for 5% -> 5% of each run, Pallas kernels for 0% -> 0%
where the time goes in v1:
time: 754 us; the launch traced here: 752 us
  waiting for transfers between devices  387 us (51%)
  blocking collectives  228 us (30%)
  matrix products  85.2 us (11%)
  other arithmetic  18.9 us (3%)
  between operations  13.1 us (2%)
  local copies, waits for them, and re-layouts  9.96 us (1%)
  starting transfers between devices  9.6 us (1%)
    all_gather x7, waiting for transfers between devices, tick(): lax.all_gather(upper_own, 'tp', axis=1, tiled=True)  280 us
    all_gather x7, blocking collectives, tick(): lax.all_gather(partial_out.reshape(block_rows, -1), 'tp')  222 us
    psum x1, waiting for transfers between devices, shards(): lax.psum(partial_in.reshape(total_tokens, -1), 'tp')  73.2 us
    dot_general x14, matrix products, contract_columns(): lax.dot_general(portion, matrix, (((1,), (1,)), ((), ())), preferred_elem...  61.2 us
    all_gather x7, waiting for transfers between devices, tick(): lax.all_gather(middle_own, 'tp', axis=1, tiled=True)  19.5 us
  transfers between devices with their start and end apart: 22, of which 22 were waited for; matrix products, arithmetic and copies ran while one was open for 5% of the time, Pallas kernels for 0%

profile of v1, /device:TPU:0, one launch (start us, length us, event | category | flops | bytes accessed | tf_op | source)
XLA Modules:
  0.0 752.5 jit_solution(16859818776599766043)
XLA Ops:
  11.2 73.2 %all-reduce.2.cloned.1.call-done = f32[512,2,64]{0,2,1:T(8,128)} async-done(((f32[512,2,64]{0,2,1:T(8,128)}), f32[512,2,64]{0,2,1:T(8,128)}) %all-reduce.2.cloned.1.call-update) | async-done | bytes 262160 | tf_op jit(solution)/shard_map/psum | solution.py:48
  84.5 654.7 %while.18 = (s32[]{:T(128)}, bf16[128,512]{1,0:T(8,128)(2,1)S(1)}, f32[2,2,2048]{2,1,0:T(2,128)S(1)}, pred[]{:T(512)}, s32[]{:T(128)}, /*index=5*/bf16[512,4096]...) while((s32[]{:T(128)}, bf16[128,512]{1,0:T(8,128)(2,1)S(1)}, ...), condition=%wide.region_3.4_spmd.clone, body=%wide.region_1.3_spmd.clone.sunk | while | flops 1096097792 | bytes 26280484 | solution.py:103
  89.4 40.3 %all-gather.3.cloned.1.call-done = bf16[128,4096]{1,0:T(8,128)(2,1)} async-done(((bf16[128,512]{1,0:T(8,128)(2,1)}), bf16[128,4096]{1,0:T(8,128)(2,1)}) %all-gather.3.cloned.1.call-update) | async-done | bytes 1048592 | tf_op jit(solution)/shard_map/while/body/eval_jaxpr/all_gather | solution.py:70
  129.7 4.7 add_convert_fusion.4
  137.5 31.7 %all_gather.35 = f32[8,128,64]{1,2,0:T(8,128)S(1)} all-gather(f32[1,128,64]{1,2,0:T(8,128)S(1)} %bitcast.83), channel_id=1, replica_groups=mesh['section'=4,'tp'=8] {'tp'}, dimensions={0}, use_global_device_ids=true | all-gather | bytes 294912 | tf_op jit(solution)/shard_map/while/body/eval_jaxpr/all_gather | solution.py:83
  183.2 40.0 %all-gather.3.cloned.1.call-done = bf16[128,4096]{1,0:T(8,128)(2,1)} async-done(((bf16[128,512]{1,0:T(8,128)(2,1)}), bf16[128,4096]{1,0:T(8,128)(2,1)}) %all-gather.3.cloned.1.call-update) | async-done | bytes 1048592 | tf_op jit(solution)/shard_map/while/body/eval_jaxpr/all_gather | solution.py:70
  223.2 4.7 add_convert_fusion.4
  231.0 31.7 %all_gather.35 = f32[8,128,64]{1,2,0:T(8,128)S(1)} all-gather(f32[1,128,64]{1,2,0:T(8,128)S(1)} %bitcast.83), channel_id=1, replica_groups=mesh['section'=4,'tp'=8] {'tp'}, dimensions={0}, use_global_device_ids=true | all-gather | bytes 294912 | tf_op jit(solution)/shard_map/while/body/eval_jaxpr/all_gather | solution.py:83
  276.7 40.0 %all-gather.3.cloned.1.call-done = bf16[128,4096]{1,0:T(8,128)(2,1)} async-done(((bf16[128,512]{1,0:T(8,128)(2,1)}), bf16[128,4096]{1,0:T(8,128)(2,1)}) %all-gather.3.cloned.1.call-update) | async-done | bytes 1048592 | tf_op jit(solution)/shard_map/while/body/eval_jaxpr/all_gather | solution.py:70
  316.7 4.7 add_convert_fusion.4
  324.5 31.7 %all_gather.35 = f32[8,128,64]{1,2,0:T(8,128)S(1)} all-gather(f32[1,128,64]{1,2,0:T(8,128)S(1)} %bitcast.83), channel_id=1, replica_groups=mesh['section'=4,'tp'=8] {'tp'}, dimensions={0}, use_global_device_ids=true | all-gather | bytes 294912 | tf_op jit(solution)/shard_map/while/body/eval_jaxpr/all_gather | solution.py:83
  370.2 40.0 %all-gather.3.cloned.1.call-done = bf16[128,4096]{1,0:T(8,128)(2,1)} async-done(((bf16[128,512]{1,0:T(8,128)(2,1)}), bf16[128,4096]{1,0:T(8,128)(2,1)}) %all-gather.3.cloned.1.call-update) | async-done | bytes 1048592 | tf_op jit(solution)/shard_map/while/body/eval_jaxpr/all_gather | solution.py:70
  410.2 4.7 add_convert_fusion.4
  418.0 31.7 %all_gather.35 = f32[8,128,64]{1,2,0:T(8,128)S(1)} all-gather(f32[1,128,64]{1,2,0:T(8,128)S(1)} %bitcast.83), channel_id=1, replica_groups=mesh['section'=4,'tp'=8] {'tp'}, dimensions={0}, use_global_device_ids=true | all-gather | bytes 294912 | tf_op jit(solution)/shard_map/while/body/eval_jaxpr/all_gather | solution.py:83
  463.7 40.0 %all-gather.3.cloned.1.call-done = bf16[128,4096]{1,0:T(8,128)(2,1)} async-done(((bf16[128,512]{1,0:T(8,128)(2,1)}), bf16[128,4096]{1,0:T(8,128)(2,1)}) %all-gather.3.cloned.1.call-update) | async-done | bytes 1048592 | tf_op jit(solution)/shard_map/while/body/eval_jaxpr/all_gather | solution.py:70
  503.7 4.7 add_convert_fusion.4
  511.5 31.7 %all_gather.35 = f32[8,128,64]{1,2,0:T(8,128)S(1)} all-gather(f32[1,128,64]{1,2,0:T(8,128)S(1)} %bitcast.83), channel_id=1, replica_groups=mesh['section'=4,'tp'=8] {'tp'}, dimensions={0}, use_global_device_ids=true | all-gather | bytes 294912 | tf_op jit(solution)/shard_map/while/body/eval_jaxpr/all_gather | solution.py:83
  557.2 40.0 %all-gather.3.cloned.1.call-done = bf16[128,4096]{1,0:T(8,128)(2,1)} async-done(((bf16[128,512]{1,0:T(8,128)(2,1)}), bf16[128,4096]{1,0:T(8,128)(2,1)}) %all-gather.3.cloned.1.call-update) | async-done | bytes 1048592 | tf_op jit(solution)/shard_map/while/body/eval_jaxpr/all_gather | solution.py:70
  597.2 4.7 add_convert_fusion.4
  605.0 31.7 %all_gather.35 = f32[8,128,64]{1,2,0:T(8,128)S(1)} all-gather(f32[1,128,64]{1,2,0:T(8,128)S(1)} %bitcast.83), channel_id=1, replica_groups=mesh['section'=4,'tp'=8] {'tp'}, dimensions={0}, use_global_device_ids=true | all-gather | bytes 294912 | tf_op jit(solution)/shard_map/while/body/eval_jaxpr/all_gather | solution.py:83
  650.7 40.0 %all-gather.3.cloned.1.call-done = bf16[128,4096]{1,0:T(8,128)(2,1)} async-done(((bf16[128,512]{1,0:T(8,128)(2,1)}), bf16[128,4096]{1,0:T(8,128)(2,1)}) %all-gather.3.cloned.1.call-update) | async-done | bytes 1048592 | tf_op jit(solution)/shard_map/while/body/eval_jaxpr/all_gather | solution.py:70
  690.7 4.7 add_convert_fusion.4
  698.5 31.7 %all_gather.35 = f32[8,128,64]{1,2,0:T(8,128)S(1)} all-gather(f32[1,128,64]{1,2,0:T(8,128)S(1)} %bitcast.83), channel_id=1, replica_groups=mesh['section'=4,'tp'=8] {'tp'}, dimensions={0}, use_global_device_ids=true | all-gather | bytes 294912 | tf_op jit(solution)/shard_map/while/body/eval_jaxpr/all_gather | solution.py:83
  739.7 6.2 psum.15
  (160 shorter events, 124.0 us)
Async XLA Ops:
  6.5 732.7 %copy-start = (bf16[2,64,2048]{2,1,0:T(8,128)(2,1)S(1)}, bf16[2,64,2048]{2,1,0:T(8,128)(2,1)}, u32[]{:S(2)}) copy-start(bf16[2,64,2048]{2,1,0:T(8,128)(2,1)} %param.13) | copy-start | bytes 1572868
  6.5 77.9 %all-reduce.2.cloned.1.call-start = ((), (), s32[]{:S(2)}) async-start(), calls=%async_computation | async-start | bytes 524288 | tf_op jit(solution)/shard_map/psum | solution.py:48
  9.2 75.2 %copy-start.4 = (s32[4]{0:T(128)S(1)}, s32[4]{0:T(128)}, u32[]{:S(2)}) copy-start(s32[4]{0:T(128)} %param.15) | copy-start | bytes 52
  84.5 45.3 %all-gather.3.cloned.1.call-start = ((), (), s32[]{:S(2)}) async-start(), calls=%async_computation.1 | async-start | bytes 1179648 | tf_op jit(solution)/shard_map/while/body/eval_jaxpr/all_gather | solution.py:70
  84.5 3.2 collective-permute-start
  89.3 84.8 %all-gather.5.cloned.1.call-start = ((), (), s32[]{:S(2)}) async-start(), calls=%async_computation.2 | async-start | bytes 1179648 | tf_op jit(solution)/shard_map/while/body/eval_jaxpr/all_gather | solution.py:74
  178.2 45.0 %all-gather.3.cloned.1.call-start = ((), (), s32[]{:S(2)}) async-start(), calls=%async_computation.1 | async-start | bytes 1179648 | tf_op jit(solution)/shard_map/while/body/eval_jaxpr/all_gather | solution.py:70
  178.3 3.2 collective-permute-start
  183.2 84.5 %all-gather.5.cloned.1.call-start = ((), (), s32[]{:S(2)}) async-start(), calls=%async_computation.2 | async-start | bytes 1179648 | tf_op jit(solution)/shard_map/while/body/eval_jaxpr/all_gather | solution.py:74
  271.7 45.0 %all-gather.3.cloned.1.call-start = ((), (), s32[]{:S(2)}) async-start(), calls=%async_computation.1 | async-start | bytes 1179648 | tf_op jit(solution)/shard_map/while/body/eval_jaxpr/all_gather | solution.py:70
  271.8 3.2 collective-permute-start
  276.7 84.5 %all-gather.5.cloned.1.call-start = ((), (), s32[]{:S(2)}) async-start(), calls=%async_computation.2 | async-start | bytes 1179648 | tf_op jit(solution)/shard_map/while/body/eval_jaxpr/all_gather | solution.py:74
  365.2 45.0 %all-gather.3.cloned.1.call-start = ((), (), s32[]{:S(2)}) async-start(), calls=%async_computation.1 | async-start | bytes 1179648 | tf_op jit(solution)/shard_map/while/body/eval_jaxpr/all_gather | solution.py:70
  365.3 3.2 collective-permute-start
  370.2 84.5 %all-gather.5.cloned.1.call-start = ((), (), s32[]{:S(2)}) async-start(), calls=%async_computation.2 | async-start | bytes 1179648 | tf_op jit(solution)/shard_map/while/body/eval_jaxpr/all_gather | solution.py:74
  458.7 45.0 %all-gather.3.cloned.1.call-start = ((), (), s32[]{:S(2)}) async-start(), calls=%async_computation.1 | async-start | bytes 1179648 | tf_op jit(solution)/shard_map/while/body/eval_jaxpr/all_gather | solution.py:70
  458.8 3.2 collective-permute-start
  463.7 84.5 %all-gather.5.cloned.1.call-start = ((), (), s32[]{:S(2)}) async-start(), calls=%async_computation.2 | async-start | bytes 1179648 | tf_op jit(solution)/shard_map/while/body/eval_jaxpr/all_gather | solution.py:74
  552.2 45.0 %all-gather.3.cloned.1.call-start = ((), (), s32[]{:S(2)}) async-start(), calls=%async_computation.1 | async-start | bytes 1179648 | tf_op jit(solution)/shard_map/while/body/eval_jaxpr/all_gather | solution.py:70
  552.3 3.2 collective-permute-start
  557.2 84.5 %all-gather.5.cloned.1.call-start = ((), (), s32[]{:S(2)}) async-start(), calls=%async_computation.2 | async-start | bytes 1179648 | tf_op jit(solution)/shard_map/while/body/eval_jaxpr/all_gather | solution.py:74
  645.7 45.0 %all-gather.3.cloned.1.call-start = ((), (), s32[]{:S(2)}) async-start(), calls=%async_computation.1 | async-start | bytes 1179648 | tf_op jit(solution)/shard_map/while/body/eval_jaxpr/all_gather | solution.py:70
  645.8 3.2 collective-permute-start
  650.7 84.5 %all-gather.5.cloned.1.call-start = ((), (), s32[]{:S(2)}) async-start(), calls=%async_computation.2 | async-start | bytes 1179648 | tf_op jit(solution)/shard_map/while/body/eval_jaxpr/all_gather | solution.py:74
  (15 other events, 156.9 us)
Sparse Core Ops, SparseCore 0:
  10.7 73.7 all-reduce.1
  89.5 40.2 all-gather.2
  134.6 39.5 all-gather.4
  183.3 39.8 all-gather.2
  228.1 39.5 all-gather.4
  276.8 39.8 all-gather.2
  321.6 39.5 all-gather.4
  370.3 39.8 all-gather.2
  415.1 39.5 all-gather.4
  463.8 39.8 all-gather.2
  508.6 39.5 all-gather.4
  557.3 39.8 all-gather.2
  602.1 39.5 all-gather.4
  650.8 39.8 all-gather.2
  695.6 39.5 all-gather.4
